TPU v7x, 256 devices: a whole 4x4x8 slice. The times are simulated.
256 devices in a mesh: replica: 64 (over y, z, core), tensor: 4 (over x).
Axes of the slice: x: 4, y: 4, z: 8, core: 2. Of those that a mesh axis runs over, the one named last changes fastest.
Arguments:
- grad_q: bfloat16 [131072, 2048], P('replica', 'tensor'), may hold values from -6 to 6
- error_q: bfloat16 [131072, 2048], P('replica', 'tensor'), may hold values from -6 to 6
- qfac_q: bfloat16 [2048, 32], P('tensor'), may hold values from -0.25 to 0.25
- ginv_q: float32 [128, 32], P('tensor'), as said below
- weight_q: float32 [2048, 2048], P('replica', 'tensor'), may hold values from -6 to 6
- momentum_q: float32 [2048, 2048], P('replica', 'tensor'), may hold values from -4 to 4
- grad_o: bfloat16 [131072, 2048], P(('replica', 'tensor')), may hold values from -6 to 6
- error_o: bfloat16 [131072, 2048], P(('replica', 'tensor')), may hold values from -6 to 6
- qfac_o: bfloat16 [8192, 32], P('tensor'), may hold values from -0.125 to 0.125
- ginv_o: float32 [128, 32], P('tensor'), as said below
- weight_o: float32 [2048, 2048], P('tensor', 'replica'), may hold values from -6 to 6
- momentum_o: float32 [2048, 2048], P('tensor', 'replica'), may hold values from -4 to 4
- norm_grads: bfloat16 [64, 4, 4096], P('replica', 'tensor'), may hold values from -24 to 24
Outputs:
- error_q_new: bfloat16 [131072, 2048], P('replica', 'tensor')
- qfac_q_new: bfloat16 [2048, 32], P('tensor')
- momentum_q_new: float32 [2048, 2048], P('replica', 'tensor')
- weight_q_new: float32 [2048, 2048], P('replica', 'tensor')
- error_o_new: bfloat16 [131072, 2048], P(('replica', 'tensor'))
- qfac_o_new: bfloat16 [8192, 32], P('tensor')
- momentum_o_new: float32 [2048, 2048], P('tensor', 'replica')
- weight_o_new: float32 [2048, 2048], P('tensor', 'replica')
- norm_mean: float32 [4096], replicated
Inputs may be any that keep to these rules, and one draw needn't show every extreme that they name: `ginv_q`: each block of 32 rows is an upper-triangular matrix with a positive diagonal. `ginv_o`: each block of 32 rows is an upper-triangular matrix with a positive diagonal.
All inputs are finite; a program needn't handle non-finite values.
Results may differ from a plain program's by a relative error of at most 0.0085.
Values may be sent and summed in bfloat16 or wider, within the bound.
A program may use at most 64 MiB of HBM per device.

v0:
```python
import jax
import jax.numpy as jnp
from jax import lax
from jax.sharding import PartitionSpec as P

momentum_decay = 0.9
step_size = 0.5


def left_factor(matrix, factor):
    return jnp.dot(matrix, factor, preferred_element_type=jnp.float32)


def right_factor(matrix, p_hat):
    return lax.dot_general(
        matrix, p_hat, (((0,), (0,)), ((), ())), preferred_element_type=jnp.float32
    )


def orthonormal(p_part, gram):
    return jnp.dot(p_part, gram, precision=lax.Precision.HIGHEST).astype(jnp.bfloat16)


def on_device(
    grad_q,
    error_q,
    qfac_q,
    ginv_q,
    weight_q,
    momentum_q,
    grad_o,
    error_o,
    qfac_o,
    ginv_o,
    weight_o,
    momentum_o,
    norm_grads,
):
    replicas = lax.axis_size("replica")
    tensors = lax.axis_size("tensor")
    mat_q = (grad_q.astype(jnp.float32) + error_q.astype(jnp.float32)).astype(jnp.bfloat16)
    mat_o = (grad_o.astype(jnp.float32) + error_o.astype(jnp.float32)).astype(jnp.bfloat16)
    p_q = left_factor(mat_q, qfac_q)
    p_o = left_factor(mat_o, qfac_o)
    norm_part = norm_grads.reshape(-1).astype(jnp.float32)
    norm_total = lax.psum(norm_part, ("replica", "tensor"))
    sum_q, sum_o = lax.psum((p_q, p_o), "replica")
    phat_q = orthonormal(sum_q, ginv_q)
    phat_o = orthonormal(sum_o, ginv_o)
    qpart_q = right_factor(mat_q, phat_q)
    qpart_o = right_factor(mat_o, phat_o)
    qsum_q, qsum_o = lax.psum((qpart_q, qpart_o), "replica")
    qnew_q = (qsum_q / replicas).astype(jnp.bfloat16)
    qnew_o = (qsum_o / replicas).astype(jnp.bfloat16)
    approx_q = lax.dot_general(
        phat_q, qnew_q, (((1,), (1,)), ((), ())), preferred_element_type=jnp.float32
    )
    approx_o = lax.dot_general(
        phat_o, qnew_o, (((1,), (1,)), ((), ())), preferred_element_type=jnp.float32
    )
    error_q_new = (mat_q.astype(jnp.float32) - approx_q).astype(jnp.bfloat16)
    error_o_new = (mat_o.astype(jnp.float32) - approx_o).astype(jnp.bfloat16)
    replica_index = lax.axis_index("replica")
    piece_rows = weight_q.shape[0]
    piece_q = lax.dynamic_slice_in_dim(approx_q, replica_index * piece_rows, piece_rows, 0)
    piece_cols = weight_o.shape[1]
    piece_o = lax.dynamic_slice_in_dim(approx_o, replica_index * piece_cols, piece_cols, 1)
    momentum_q_new = momentum_decay * momentum_q + piece_q
    weight_q_new = weight_q - step_size * momentum_q_new
    momentum_o_new = momentum_decay * momentum_o + piece_o
    weight_o_new = weight_o - step_size * momentum_o_new
    norm_mean = norm_total / (replicas * tensors)
    return (
        error_q_new,
        qnew_q,
        momentum_q_new,
        weight_q_new,
        error_o_new,
        qnew_o,
        momentum_o_new,
        weight_o_new,
        norm_mean,
    )


def solution(mesh):
    in_specs = (
        P("replica", "tensor"),
        P("replica", "tensor"),
        P("tensor", None),
        P("tensor", None),
        P("replica", "tensor"),
        P("replica", "tensor"),
        P(("replica", "tensor"), None),
        P(("replica", "tensor"), None),
        P("tensor", None),
        P("tensor", None),
        P("tensor", "replica"),
        P("tensor", "replica"),
        P("replica", "tensor", None),
    )
    out_specs = (
        P("replica", "tensor"),
        P("tensor", None),
        P("replica", "tensor"),
        P("replica", "tensor"),
        P(("replica", "tensor"), None),
        P("tensor", None),
        P("tensor", "replica"),
        P("tensor", "replica"),
        P(),
    )
    return jax.shard_map(
        on_device, mesh=mesh, in_specs=in_specs, out_specs=out_specs, check_vma=False
    )
```

profile of v0, /device:TPU:1, one launch (start us, length us, event | category | flops | bytes accessed | tf_op | source)
XLA Modules:
  0.0 407.3 jit_solution(12464076429160875396)
XLA Ops:
  7.2 0.0 copy-start
  7.2 0.0 copy-start.1
  7.2 0.0 all-reduce.7.cloned.1.call-start
  7.2 0.0 copy-start.2
  7.3 4.0 fusion.1
  11.3 0.0 copy-done
  11.3 0.0 copy-done.1
  11.3 0.0 copy-done.2
  11.3 0.0 copy-start.8
  11.3 0.0 copy-start.9
  11.3 0.0 copy-start.15
  11.3 0.0 copy-start.14
  11.4 1.4 fusion.3
  12.8 0.0 all-reduce.7.cloned.1.call-update
  12.8 0.0 all-reduce.5.cloned.1.call-start
  12.9 0.0 copy-done.8
  12.9 0.1 copy.22
  13.0 0.0 copy-done.9
  13.0 0.1 copy.23
  13.1 0.0 copy-done.15
  13.2 82.0 %psum.39 = f32[4096]{0:T(1024)S(1)} all-reduce(f32[4096]{0:T(1024)S(1)} %bitcast.13), channel_id=1, replica_groups=mesh['replica'=64,'tensor'=4] {'replica','tensor'}, use_global_device_ids=true, to_apply=%region_4.0 | all-reduce | flops 4096 | bytes 32768 | tf_op jit(solution)/shard_map/psum | solution.py:46
  95.2 107.8 %all-reduce.7.cloned.1.call-done = (f32[2048,32]{1,0:T(8,128)}, f32[512,32]{1,0:T(8,128)}) async-done(((f32[2048,32]{1,0:T(8,128)}, f32[512,32]{1,0:T(8,128)}), (f32[2048,32]{1,0:T(8,128)}, f32[512,32]{1,0:T(8,128)})) %all-reduce.7.cloned.1.call-update) | async-done | bytes 327696 | tf_op jit(solution)/shard_map/psum | solution.py:47
  202.9 0.0 copy-done.14
  203.0 1.4 convolution_convert_fusion.1
  204.4 0.0 copy-start.3
  204.4 0.0 copy-start.4
  204.4 3.1 fusion.2
  207.5 0.0 copy-done.5
  207.5 0.0 copy-done.13
  207.5 1.2 convolution_convert_fusion
  208.8 0.0 copy-done.3
  208.8 1.3 fusion
  210.1 0.0 all-reduce.5.cloned.1.call-update
  210.1 0.6 broadcast_multiply_fusion
  210.7 178.3 %all-reduce.5.cloned.1.call-done = (f32[512,32]{0,1:T(8,128)}, f32[2048,32]{0,1:T(8,128)}) async-done(((f32[512,32]{0,1:T(8,128)}, f32[2048,32]{0,1:T(8,128)}), (f32[512,32]{0,1:T(8,128)}, f32[2048,32]{0,1:T(8,128)})) %all-reduce.5.cloned.1.call-update) | async-done | bytes 327696 | tf_op jit(solution)/shard_map/psum | solution.py:52
  389.0 1.0 multiply_convert_fusion
  390.0 0.0 copy-start.6
  390.0 3.7 subtract_convert_fusion
  393.7 0.0 copy-done.6
  393.8 0.1 multiply_subtract_fusion
  393.9 0.7 copy.24
  394.6 0.7 copy.25
  395.4 0.0 copy-start.7
  395.4 0.0 copy-start.10
  395.4 0.0 copy-start.11
  395.4 4.4 %subtract_convert_fusion.1 = (bf16[2048,512]{1,0:T(8,128)(2,1)}, f32[2048,512]{1,0:T(8,128)S(1)}) fusion(bf16[2048,512]{1,0:T(8,128)(2,1)} %param.14, bf16[2048,512]{1,0:T(8,128)(2,1)} %param.13, bf16[2048,32]{0,1:T(8,128)(2,1)S(1)} %convolution_convert_fusion, bf16[512,32]{0,1:T(8,128)(2,1)S(1)} %multiply_convert_fusion.1), kind=kOutput, calls=%fused_computation.2 | convolution fusion | flops 74448896 | bytes 10649600 | tf_op jit(solution)/shard_map/dot_general | solution.py:55
  399.8 0.0 copy-done.11
  399.8 0.7 multiply_subtract_fusion.1
  (9 shorter events, 0.0 us)
Async XLA Ops:
  7.2 4.1 %copy-start = (bf16[2048,32]{0,1:T(8,128)(2,1)S(1)}, bf16[2048,32]{0,1:T(8,128)(2,1)}, u32[]{:S(2)}) copy-start(bf16[2048,32]{0,1:T(8,128)(2,1)} %param.21) | copy-start | bytes 393220
  7.2 4.1 %copy-start.1 = (bf16[512,2048]{1,0:T(8,128)(2,1)S(1)}, bf16[512,2048]{1,0:T(8,128)(2,1)}, u32[]{:S(2)}) copy-start(bf16[512,2048]{1,0:T(8,128)(2,1)} %param.20) | copy-start | bytes 6291460
  7.2 195.7 %all-reduce.7.cloned.1.call-start = ((), (), s32[]{:S(2)}) async-start(), calls=%async_computation.1 | async-start | bytes 2621440 | tf_op jit(solution)/shard_map/psum | solution.py:47
  7.2 4.1 copy-start.2
  11.3 1.6 copy-start.8
  11.3 1.7 copy-start.9
  11.3 1.8 copy-start.15
  11.3 191.6 %copy-start.14 = (f32[32,32]{1,0:T(8,128)S(1)}, f32[32,32]{1,0:T(8,128)}, u32[]{:S(2)}) copy-start(f32[32,32]{1,0:T(8,128)} %param.22) | copy-start | bytes 12292
  12.8 376.2 %all-reduce.5.cloned.1.call-start = ((), (), s32[]{:S(2)}) async-start(), calls=%async_computation | async-start | bytes 655360 | tf_op jit(solution)/shard_map/psum | solution.py:52
  202.9 4.6 %copy-start.5 = (f32[2048,32]{1,0:T(8,128)S(1)}, f32[2048,32]{1,0:T(8,128)}, u32[]{:S(2)}) copy-start(f32[2048,32]{1,0:T(8,128)} %get-tuple-element.20) | copy-start | bytes 786436
  203.0 4.6 %copy-start.13 = (f32[32,32]{1,0:T(8,128)S(1)}, f32[32,32]{1,0:T(8,128)}, u32[]{:S(2)}) copy-start(f32[32,32]{1,0:T(8,128)} %param.16) | copy-start | bytes 12292
  204.4 4.4 %copy-start.3 = (bf16[2048,512]{1,0:T(8,128)(2,1)S(1)}, bf16[2048,512]{1,0:T(8,128)(2,1)}, u32[]{:S(2)}) copy-start(bf16[2048,512]{1,0:T(8,128)(2,1)} %param.14) | copy-start | bytes 6291460
  204.4 4.4 %copy-start.4 = (bf16[2048,512]{1,0:T(8,128)(2,1)S(1)}, bf16[2048,512]{1,0:T(8,128)(2,1)}, u32[]{:S(2)}) copy-start(bf16[2048,512]{1,0:T(8,128)(2,1)} %param.13) | copy-start | bytes 6291460
  390.0 3.8 copy-start.6
  390.0 5.4 %copy-start.12 = (f32[512,32]{0,1:T(8,128)S(1)}, f32[512,32]{0,1:T(8,128)}, u32[]{:S(2)}) copy-start(f32[512,32]{0,1:T(8,128)} %get-tuple-element.18) | copy-start | bytes 196612
  395.4 4.4 %copy-start.7 = (bf16[512,32]{0,1:T(8,128)(2,1)}, bf16[512,32]{0,1:T(8,128)(2,1)S(1)}, u32[]{:S(2)}) copy-start(bf16[512,32]{0,1:T(8,128)(2,1)S(1)} %multiply_convert_fusion.1) | copy-start | bytes 98308
  395.4 4.4 %copy-start.10 = (f32[32,512]{1,0:T(8,128)S(1)}, f32[32,512]{1,0:T(8,128)}, u32[]{:S(2)}) copy-start(f32[32,512]{1,0:T(8,128)} %param.17) | copy-start | bytes 196612
  395.4 4.4 %copy-start.11 = (f32[32,512]{1,0:T(8,128)S(1)}, f32[32,512]{1,0:T(8,128)}, u32[]{:S(2)}) copy-start(f32[32,512]{1,0:T(8,128)} %param.18) | copy-start | bytes 196612
Sparse Core Ops, SparseCore 0:
  12.9 189.9 all-reduce.6
  210.2 178.7 all-reduce.4
where the time goes:
time: 408 us; the launch traced here: 407 us
  waiting for transfers between devices  286 us (70%)
  blocking collectives  82 us (20%)
  matrix products  20.6 us (5%)
  between operations  14.3 us (4%)
    psum x1, waiting for transfers between devices, on_device(): qsum_q, qsum_o = lax.psum((qpart_q, qpart_o), 'replica')  178 us
    psum x1, waiting for transfers between devices, on_device(): sum_q, sum_o = lax.psum((p_q, p_o), 'replica')  108 us
    psum x1, blocking collectives, on_device(): norm_total = lax.psum(norm_part, ('replica', 'tensor'))  82 us
  transfers between devices with their start and end apart: 2, of which 2 were waited for; matrix products, arithmetic and copies ran while one was open for 0% of the time, Pallas kernels for 0%

commit v1 on v0

v1 whole, which is shorter than its diff:
```python
import functools

import jax
import jax.numpy as jnp
from jax import lax
from jax.experimental import pallas as pl
from jax.experimental.pallas import tpu as pltpu
from jax.sharding import PartitionSpec as P

momentum_decay = 0.9
step_size = 0.5

NY, NZ, NC = 4, 8, 2
NA = NY * NC
RANK = 32
TILES = 5
MESH = pl.DeviceIdType.MESH
f32 = jnp.float32
bf16 = jnp.bfloat16

A_FAR = [(2, 0), (2, 1), (1, 0), (3, 0), (1, 1), (3, 1), (0, 1)]
A_NEAR = A_FAR[::-1]
Z_FAR = [4, 3, 5, 2, 6, 1, 7]


def fold_gram(gram, factor_t):
    w = lax.dot_general(
        gram,
        factor_t.astype(f32),
        (((0,), (0,)), ((), ())),
        precision=lax.Precision.HIGHEST,
        preferred_element_type=f32,
    )
    w1 = w.astype(bf16)
    r1 = w - w1.astype(f32)
    w2 = r1.astype(bf16)
    w3 = (r1 - w2.astype(f32)).astype(bf16)
    return w1, w2, w3


def project(w, mat):
    out = lax.dot_general(w, mat, (((1,), (1,)), ((), ())), preferred_element_type=f32)
    return out[0:RANK] + out[RANK : 2 * RANK] + out[2 * RANK : 3 * RANK]


def wide_tiles(chunk):
    return [chunk[h * 16 : h * 16 + 16, j * 128 : j * 128 + 128] for h in range(2) for j in range(2)]


def reduce_kernel(
    replicas,
    all_devices,
    gq,
    eq,
    go,
    eo,
    fq,
    fo,
    giq,
    gio,
    nrm,
    matq_out,
    mato_out,
    gp_out,
    gn_out,
    norm_out,
    gq_v,
    eq_v,
    go_v,
    eo_v,
    mq,
    mo,
    fq_v,
    fo_v,
    giq_v,
    gio_v,
    nrm_v,
    wq,
    wo,
    send_a,
    recv_a,
    zbuf,
    gath,
    nsrc,
    nrecv,
    nz,
    nx,
    ng,
    sem_q,
    sem_o,
    sem_s,
    sem_w,
    sem_as,
    sem_ar,
    sem_zs,
    sem_zr,
    sem_gs,
    sem_gr,
    nsem_as,
    nsem_ar,
    nsem_zs,
    nsem_zr,
    nsem_xs,
    nsem_xr,
    nsem_gs,
    nsem_gr,
):
    rep = lax.axis_index("replica")
    ten = lax.axis_index("tensor")
    nx_size = lax.axis_size("tensor")
    y = rep // (NZ * NC)
    z = (rep // NC) % NZ
    core = rep % NC
    a = y * NC + core

    def a_peer(off):
        py, pc = (y + off[0]) % NY, (core + off[1]) % NC
        return py * NC + pc, ((py * NZ + z) * NC + pc, ten)

    def z_peer(dz):
        pz = (z + dz) % NZ
        return pz, ((y * NZ + pz) * NC + core, ten)

    def x_peer(dx):
        px = (ten + dx) % nx_size
        return px, (rep, px)

    barrier = pltpu.get_barrier_semaphore()
    for off in A_FAR:
        pl.semaphore_signal(barrier, inc=1, device_id=a_peer(off)[1], device_id_type=MESH)
    for dz in Z_FAR:
        pl.semaphore_signal(barrier, inc=1, device_id=z_peer(dz)[1], device_id_type=MESH)
    for dx in range(1, nx_size):
        pl.semaphore_signal(barrier, inc=1, device_id=x_peer(dx)[1], device_id_type=MESH)

    small = [(fq, fq_v), (fo, fo_v), (giq, giq_v), (gio, gio_v), (nrm, nrm_v)]
    small_copies = [pltpu.make_async_copy(s, d, sem_s.at[i]) for i, (s, d) in enumerate(small)]
    for c in small_copies:
        c.start()
    o_rows = go.shape[0] // 4
    q_rows = gq.shape[0] // NA

    def o_loads(j):
        rows = pl.ds(j * o_rows, o_rows)
        return [
            pltpu.make_async_copy(go.at[rows, :], go_v.at[rows, :], sem_o.at[0, j]),
            pltpu.make_async_copy(eo.at[rows, :], eo_v.at[rows, :], sem_o.at[1, j]),
        ]

    def q_slice(d):
        return pl.ds(pl.multiple_of(d * q_rows, q_rows), q_rows)

    def q_loads(d):
        rows = q_slice(d)
        return [
            pltpu.make_async_copy(gq.at[rows, :], gq_v.at[rows, :], sem_q.at[0, d]),
            pltpu.make_async_copy(eq.at[rows, :], eq_v.at[rows, :], sem_q.at[1, d]),
        ]

    order = A_FAR + [(0, 0)]
    for j in range(4):
        for c in o_loads(j):
            c.start()
    for off in order:
        for c in q_loads(a_peer(off)[0]):
            c.start()

    def exchange(src, dst, send_sem, recv_sem, device):
        return pltpu.make_async_remote_copy(
            src_ref=src, dst_ref=dst, send_sem=send_sem, recv_sem=recv_sem,
            device_id=device, device_id_type=MESH,
        )

    def a_copy(ph, off):
        d, dev = a_peer(off)
        return exchange(send_a.at[ph, d], recv_a.at[ph, a], sem_as.at[ph, d], sem_ar.at[ph, a], dev)

    def a_wait(ph, off):
        d, dev = a_peer(off)
        exchange(send_a.at[ph, d], recv_a.at[ph, d], sem_as.at[ph, d], sem_ar.at[ph, d], dev).wait_recv()
        return recv_a[ph, d].astype(f32)

    def z_copy(ph, dz):
        d, dev = z_peer(dz)
        return exchange(zbuf.at[ph, z], zbuf.at[ph, z], sem_zs.at[ph, d], sem_zr.at[ph, z], dev)

    def z_wait(ph, dz):
        d, dev = z_peer(dz)
        exchange(zbuf.at[ph, d], zbuf.at[ph, d], sem_zs.at[ph, d], sem_zr.at[ph, d], dev).wait_recv()

    def g_copy(ph, off):
        d, dev = a_peer(off)
        return exchange(gath.at[ph, a], gath.at[ph, a], sem_gs.at[ph, d], sem_gr.at[ph, a], dev)

    def g_wait(ph, off):
        d, dev = a_peer(off)
        exchange(gath.at[ph, d], gath.at[ph, d], sem_gs.at[ph, d], sem_gr.at[ph, d], dev).wait_recv()
        return d

    def na_copy(off):
        d, dev = a_peer(off)
        return exchange(nsrc.at[d], nrecv.at[a], nsem_as.at[d], nsem_ar.at[a], dev)

    def na_wait(off):
        d, dev = a_peer(off)
        exchange(nsrc.at[d], nrecv.at[d], nsem_as.at[d], nsem_ar.at[d], dev).wait_recv()
        return nrecv[d]

    def nz_copy(dz):
        d, dev = z_peer(dz)
        return exchange(nz.at[z], nz.at[z], nsem_zs.at[d], nsem_zr.at[z], dev)

    def nz_wait(dz):
        d, dev = z_peer(dz)
        exchange(nz.at[d], nz.at[d], nsem_zs.at[d], nsem_zr.at[d], dev).wait_recv()

    def nx_copy(dx):
        d, dev = x_peer(dx)
        return exchange(nx.at[ten], nx.at[ten], nsem_xs.at[d], nsem_xr.at[ten], dev)

    def nx_wait(dx):
        d, dev = x_peer(dx)
        exchange(nx.at[d], nx.at[d], nsem_xs.at[d], nsem_xr.at[d], dev).wait_recv()

    def ng_copy(off):
        d, dev = a_peer(off)
        return exchange(ng.at[a], ng.at[a], nsem_gs.at[d], nsem_gr.at[a], dev)

    def ng_wait(off):
        d, dev = a_peer(off)
        exchange(ng.at[d], ng.at[d], nsem_gs.at[d], nsem_gr.at[d], dev).wait_recv()

    for c in small_copies:
        c.wait()
    for i, w in enumerate(fold_gram(gio_v[...], fo_v[...])):
        wo[i * RANK : (i + 1) * RANK, :] = w
    for i, w in enumerate(fold_gram(giq_v[...], fq_v[...])):
        wq[i * RANK : (i + 1) * RANK, :] = w
    piece = nsrc.shape[2]
    for d in range(NA):
        nsrc[d] = nrm_v[0, :, d * piece : (d + 1) * piece].astype(f32)

    stores = []
    for j in range(4):
        for c in o_loads(j):
            c.wait()
        rows = pl.ds(j * o_rows, o_rows)
        mat = (go_v[rows, :].astype(f32) + eo_v[rows, :].astype(f32)).astype(bf16)
        mo[rows, :] = mat
        part = project(wo[...], mat).astype(bf16)
        send_a[0, j, 4] = part[0:16]
        send_a[0, 4 + j, 4] = part[16:32]
        c = pltpu.make_async_copy(mo.at[rows, :], mato_out.at[rows, :], sem_w.at[1, j])
        c.start()
        stores.append(c)

    n_others = len(A_FAR) + len(Z_FAR) + nx_size - 1
    pl.semaphore_wait(barrier, n_others)
    for off in A_FAR:
        na_copy(off).start()

    for off in order:
        d, _ = a_peer(off)
        for c in q_loads(d):
            c.wait()
        rows = q_slice(d)
        mat = (gq_v[rows, :].astype(f32) + eq_v[rows, :].astype(f32)).astype(bf16)
        mq[rows, :] = mat
        part = project(wq[...], mat).astype(bf16)
        for t, tile in enumerate(wide_tiles(part)):
            send_a[0, d, t] = tile
        if off != (0, 0):
            a_copy(0, off).start()
        c = pltpu.make_async_copy(mq.at[rows, :], matq_out.at[rows, :], sem_w.at[0, d])
        c.start()
        stores.append(c)

    def sum_a(ph):
        total = send_a[ph, a].astype(f32)
        for off in A_NEAR:
            total = total + a_wait(ph, off)
        zbuf[ph, z] = total.astype(bf16)
        for dz in Z_FAR:
            z_copy(ph, dz).start()

    def sum_z(ph, divisor):
        for dz in Z_FAR[::-1]:
            z_wait(ph, dz)
        total = zbuf[ph, 0].astype(f32)
        for k in range(1, NZ):
            total = total + zbuf[ph, k].astype(f32)
        if divisor is not None:
            total = total / divisor
        gath[ph, a] = total.astype(bf16)
        for off in A_FAR:
            g_copy(ph, off).start()

    ntotal = nsrc[a]
    for off in A_NEAR:
        ntotal = ntotal + na_wait(off)
    nz[z] = ntotal
    for dz in Z_FAR:
        nz_copy(dz).start()

    sum_a(0)

    for dz in Z_FAR:
        nz_wait(dz)
    ntotal = nz[0]
    for k in range(1, NZ):
        ntotal = ntotal + nz[k]
    nx[ten] = ntotal
    for dx in range(1, nx_size):
        nx_copy(dx).start()

    sum_z(0, None)

    for dx in range(1, nx_size):
        nx_wait(dx)
    ntotal = nx[0]
    for k in range(1, nx_size):
        ntotal = ntotal + nx[k]
    ng[a] = ntotal / all_devices
    for off in A_FAR:
        ng_copy(off).start()

    acc_q = jnp.zeros((RANK, mq.shape[1]), f32)
    for off in [(0, 0)] + A_NEAR:
        d = a if off == (0, 0) else g_wait(0, off)
        left = jnp.concatenate(
            [
                jnp.concatenate([gath[0, d, 0], gath[0, d, 1]], axis=1),
                jnp.concatenate([gath[0, d, 2], gath[0, d, 3]], axis=1),
            ],
            axis=0,
        )
        acc_q = acc_q + jnp.dot(left, mq[q_slice(d), :], preferred_element_type=f32)
    for d in range(NA):
        h, j = d // 4, d % 4
        send_a[1, d, 4] = acc_q[h * 16 : h * 16 + 16, j * 128 : j * 128 + 128].astype(bf16)
    left = jnp.concatenate(
        [jnp.concatenate([gath[0, 4 * h + j, 4] for j in range(4)], axis=1) for h in range(2)], axis=0
    )
    o_cols = mo.shape[1] // NA
    for off in order:
        d, _ = a_peer(off)
        cols = pl.ds(pl.multiple_of(d * o_cols, o_cols), o_cols)
        part = jnp.dot(left, mo[:, cols], preferred_element_type=f32).astype(bf16)
        for t, tile in enumerate(wide_tiles(part)):
            send_a[1, d, t] = tile
        if off != (0, 0):
            a_copy(1, off).start()
    gp_out[...] = gath[0]

    sum_a(1)
    for off in A_FAR:
        ng_wait(off)
    for d in range(NA):
        norm_out[:, d * piece : (d + 1) * piece] = ng[d]
    sum_z(1, replicas)
    for c in stores:
        c.wait()
    for ph in range(2):
        for off in A_FAR:
            a_copy(ph, off).wait_send()
        for dz in Z_FAR:
            z_copy(ph, dz).wait_send()
    for off in A_FAR:
        g_copy(0, off).wait_send()
        na_copy(off).wait_send()
        ng_copy(off).wait_send()
    for dz in Z_FAR:
        nz_copy(dz).wait_send()
    for dx in range(1, nx_size):
        nx_copy(dx).wait_send()
    for off in A_NEAR:
        g_wait(1, off)
    gn_out[...] = gath[1]
    for off in A_FAR:
        g_copy(1, off).wait_send()


def wide(ref, d):
    return jnp.concatenate(
        [
            jnp.concatenate([ref[d, 0], ref[d, 1]], axis=1),
            jnp.concatenate([ref[d, 2], ref[d, 3]], axis=1),
        ],
        axis=0,
    )


def narrow(ref):
    return jnp.concatenate(
        [jnp.concatenate([ref[4 * h + j, 4] for j in range(4)], axis=1) for h in range(2)], axis=0
    )


def outer(left_t, right_t):
    return lax.dot_general(left_t, right_t, (((0,), (0,)), ((), ())), preferred_element_type=f32)


def update_kernel(
    gp, gn, nrm, mq, mo, wq, mom_q, wo, mom_o,
    eq_out, eo_out, fq_out, fo_out, momq_out, wq_out, momo_out, wo_out, norm_out,
    turn,
):
    s = pl.program_id(0)
    rep = lax.axis_index("replica")
    right_q = narrow(gn)

    @pl.when(s == 0)
    def _():
        fq_out[...] = right_q
        for d in range(NA):
            fo_out[:, d * 256 : (d + 1) * 256] = wide(gn, d)
        norm_out[...] = nrm[...]
        c = rep // 8
        off = pl.multiple_of((rep % 8) * RANK, RANK)
        turn[...] = wide(gp, c).astype(f32).T
        left = turn[pl.ds(off, RANK), :].astype(bf16)
        piece = jnp.dot(left, right_q, preferred_element_type=f32)
        m = momentum_decay * mom_q[...] + piece
        momq_out[...] = m
        wq_out[...] = wq[...] - step_size * m
        turn[...] = wide(gn, c).astype(f32).T
        left = turn[pl.ds(off, RANK), :].astype(bf16)
        piece = jnp.dot(left, narrow(gp), preferred_element_type=f32)
        m = momentum_decay * mom_o[...] + piece
        momo_out[...] = m
        wo_out[...] = wo[...] - step_size * m

    for k in range(2):
        rows = slice(k * 256, (k + 1) * 256)
        approx = outer(wide(gp, 2 * s + k), right_q)
        eq_out[rows, :] = (mq[rows, :].astype(f32) - approx).astype(bf16)
    left_o = jnp.concatenate([gp[s, 4], gp[4 + s, 4]], axis=0)
    for d in range(NA):
        cols = slice(d * 256, (d + 1) * 256)
        approx = outer(left_o, wide(gn, d))
        eo_out[:, cols] = (mo[:, cols].astype(f32) - approx).astype(bf16)


def on_device(
    grad_q,
    error_q,
    qfac_q,
    ginv_q,
    weight_q,
    momentum_q,
    grad_o,
    error_o,
    qfac_o,
    ginv_o,
    weight_o,
    momentum_o,
    norm_grads,
):
    replicas = lax.axis_size("replica")
    tensors = lax.axis_size("tensor")
    shape_q, shape_o = grad_q.shape, grad_o.shape
    piece = norm_grads.shape[2] // NA
    packed = (NA, TILES, 16, 128)
    any_spec = pl.BlockSpec(memory_space=pl.ANY)
    vmem_spec = pl.BlockSpec(memory_space=pltpu.VMEM)
    dma = pltpu.SemaphoreType.DMA
    mat_q, mat_o, gp, gn, norm = pl.pallas_call(
        functools.partial(reduce_kernel, replicas, replicas * tensors),
        out_shape=(
            jax.ShapeDtypeStruct(shape_q, bf16),
            jax.ShapeDtypeStruct(shape_o, bf16),
            jax.ShapeDtypeStruct(packed, bf16),
            jax.ShapeDtypeStruct(packed, bf16),
            jax.ShapeDtypeStruct((1, NA * piece), f32),
        ),
        in_specs=[any_spec] * 9,
        out_specs=(any_spec, any_spec, vmem_spec, vmem_spec, vmem_spec),
        scratch_shapes=[
            pltpu.VMEM(shape_q, bf16),
            pltpu.VMEM(shape_q, bf16),
            pltpu.VMEM(shape_o, bf16),
            pltpu.VMEM(shape_o, bf16),
            pltpu.VMEM(shape_q, bf16),
            pltpu.VMEM(shape_o, bf16),
            pltpu.VMEM((RANK, shape_q[1]), bf16),
            pltpu.VMEM((RANK, shape_o[1]), bf16),
            pltpu.VMEM((RANK, RANK), f32),
            pltpu.VMEM((RANK, RANK), f32),
            pltpu.VMEM(norm_grads.shape, bf16),
            pltpu.VMEM((3 * RANK, shape_q[1]), bf16),
            pltpu.VMEM((3 * RANK, shape_o[1]), bf16),
            pltpu.VMEM((2,) + packed, bf16),
            pltpu.VMEM((2,) + packed, bf16),
            pltpu.VMEM((2,) + packed, bf16),
            pltpu.VMEM((2,) + packed, bf16),
            pltpu.VMEM((NA, 1, piece), f32),
            pltpu.VMEM((NA, 1, piece), f32),
            pltpu.VMEM((NZ, 1, piece), f32),
            pltpu.VMEM((tensors, 1, piece), f32),
            pltpu.VMEM((NA, 1, piece), f32),
            dma((2, NA)),
            dma((2, 4)),
            dma((5,)),
            dma((2, NA)),
            dma((2, NA)),
            dma((2, NA)),
            dma((2, NZ)),
            dma((2, NZ)),
            dma((2, NA)),
            dma((2, NA)),
            dma((NA,)),
            dma((NA,)),
            dma((NZ,)),
            dma((NZ,)),
            dma((tensors,)),
            dma((tensors,)),
            dma((NA,)),
            dma((NA,)),
        ],
        compiler_params=pltpu.CompilerParams(collective_id=0, has_side_effects=True),
        name="reduce_factors",
    )(grad_q, error_q, grad_o, error_o, qfac_q.T, qfac_o.T, ginv_q, ginv_o, norm_grads)

    steps = 4
    whole = lambda shape: pl.BlockSpec(shape, lambda s: (0,) * len(shape))
    rows_q, rows_o = shape_q[0] // steps, shape_o[0] // steps
    block_q = pl.BlockSpec((rows_q, shape_q[1]), lambda s: (s, 0))
    block_o = pl.BlockSpec((rows_o, shape_o[1]), lambda s: (s, 0))
    wide_piece = (RANK, shape_q[1])
    outs = pl.pallas_call(
        update_kernel,
        grid=(steps,),
        out_shape=(
            jax.ShapeDtypeStruct(shape_q, bf16),
            jax.ShapeDtypeStruct(shape_o, bf16),
            jax.ShapeDtypeStruct((RANK, shape_q[1]), bf16),
            jax.ShapeDtypeStruct((RANK, shape_o[1]), bf16),
            jax.ShapeDtypeStruct(wide_piece, f32),
            jax.ShapeDtypeStruct(wide_piece, f32),
            jax.ShapeDtypeStruct(wide_piece, f32),
            jax.ShapeDtypeStruct(wide_piece, f32),
            jax.ShapeDtypeStruct((1, NA * piece), f32),
        ),
        in_specs=[
            whole(packed),
            whole(packed),
            whole((1, NA * piece)),
            block_q,
            block_o,
            whole(wide_piece),
            whole(wide_piece),
            whole(wide_piece),
            whole(wide_piece),
        ],
        out_specs=(
            block_q,
            block_o,
            whole((RANK, shape_q[1])),
            whole((RANK, shape_o[1])),
            whole(wide_piece),
            whole(wide_piece),
            whole(wide_piece),
            whole(wide_piece),
            whole((1, NA * piece)),
        ),
        scratch_shapes=[pltpu.VMEM((256, RANK), f32)],
        name="apply_update",
    )(gp, gn, norm, mat_q, mat_o, weight_q, momentum_q, weight_o.T, momentum_o.T)
    error_q_new, error_o_new, fq_t, fo_t, momq, wq, momo_t, wo_t, norm_mean = outs
    return (
        error_q_new,
        fq_t.T,
        momq,
        wq,
        error_o_new,
        fo_t.T,
        momo_t.T,
        wo_t.T,
        norm_mean.reshape(-1),
    )


def solution(mesh):
    in_specs = (
        P("replica", "tensor"),
        P("replica", "tensor"),
        P("tensor", None),
        P("tensor", None),
        P("replica", "tensor"),
        P("replica", "tensor"),
        P(("replica", "tensor"), None),
        P(("replica", "tensor"), None),
        P("tensor", None),
        P("tensor", None),
        P("tensor", "replica"),
        P("tensor", "replica"),
        P("replica", "tensor", None),
    )
    out_specs = (
        P("replica", "tensor"),
        P("tensor", None),
        P("replica", "tensor"),
        P("replica", "tensor"),
        P(("replica", "tensor"), None),
        P("tensor", None),
        P("tensor", "replica"),
        P("tensor", "replica"),
        P(),
    )
    return jax.shard_map(
        on_device, mesh=mesh, in_specs=in_specs, out_specs=out_specs, check_vma=False
    )
```

time: 408 us -> 50.8 us (0.12)
  waiting for transfers between devices: 286 us -> 0 us
  blocking collectives: 82 us -> 0 us
  Pallas kernels: 0 us -> 50 us
  matrix products: 20.6 us -> 0 us
  between operations: 14.3 us -> 0.65 us
    psum x2 -> x0, waiting for transfers between devices: 286 us -> none  [the longest x1 178 us: on_device(): qsum_q, qsum_o = lax.psum((qpart_q, qpart_o), 'replica')]
    psum x1 -> x0, blocking collectives: 82 us -> none  [on_device(): norm_total = lax.psum(norm_part, ('replica', 'tensor'))]
    pallas_call x0 -> x2, Pallas kernels: none -> 50 us  [the longest x1 44.2 us: on_device(): pl.pallas_call(functools.partial(reduce_kernel, replicas, replicas * tens...]
    dot_general x8 -> x0, matrix products: 20.6 us -> none  [the longest x2 5.46 us: left_factor(): return jnp.dot(matrix, factor, preferred_element_type=jnp.float32)]
  transfers between devices with their start and end apart: 2 -> 0, of which waited for: 2 -> 0; matrix products, arithmetic and copies ran while one was open for 0% -> 0% of each run, Pallas kernels for 0% -> 0%
where the time goes in v1:
time: 50.8 us; the launch traced here: 50.7 us
  Pallas kernels  50 us (98%)
  between operations  0.65 us (1%)
    pallas_call x1, Pallas kernels, on_device(): pl.pallas_call(functools.partial(reduce_kernel, replicas, replicas * tens...  44.2 us
    pallas_call x1, Pallas kernels, on_device(): pl.pallas_call(update_kernel, grid=(steps,), out_shape=(jax.ShapeDtypeStr...  5.81 us

profile of v1, /device:TPU:1, one launch (start us, length us, event | category | flops | bytes accessed | tf_op | source)
XLA Modules:
  0.0 50.7 jit_solution(4825033169819314371)
XLA Ops:
  0.6 44.2 %reduce_factors.1 = (bf16[2048,512]{1,0:T(8,128)(2,1)}, bf16[512,2048]{1,0:T(8,128)(2,1)}, bf16[8,5,16,128]{3,2,1,0:T(8,128)(2,1)}, bf16[8,5,16,128]{3,2,1,0:T(8,128)(2,1)}, f32[1,4096]{1,0:T(1,128)}) custom-call(bf16[2048,512]{1,0:T(8,128)(2,1)} %gq.1, bf16[2048,512]{1,0:T(8,128)(2,1)} %eq.1, bf16[512,2048]{1,0:T(8,128)(2,1)} %go.1, bf16[512,2048]{1,0:T(8,128)(2,1)} %eo.1, ...), custom_call_target="tpu_custom_call" | custom-call | tf_op jit(solution)/shard_map/reduce_factors/pallas_call | solution.py:467
  44.9 5.8 %apply_update.1 = (bf16[2048,512]{1,0:T(8,128)(2,1)}, bf16[512,2048]{1,0:T(8,128)(2,1)}, bf16[32,512]{1,0:T(8,128)(2,1)}, bf16[32,2048]{1,0:T(8,128)(2,1)}, f32[...) custom-call(bf16[8,5,16,128]{3,2,1,0:T(8,128)(2,1)} %get-tuple-element.23.g, ...), custom_call_target="tpu_custom_call" | custom-call | tf_op jit(solution)/shard_map/apply_update/pallas_call | solution.py:530

commit v2 on v1

v2 whole, which is shorter than its diff:
```python
import functools

import jax
import jax.numpy as jnp
from jax import lax
from jax.experimental import pallas as pl
from jax.experimental.pallas import tpu as pltpu
from jax.sharding import PartitionSpec as P

momentum_decay = 0.9
step_size = 0.5

NY, NZ, NC = 4, 8, 2
NA = NY * NC
RANK = 32
TILES = 5
MESH = pl.DeviceIdType.MESH
f32 = jnp.float32
bf16 = jnp.bfloat16

A_FAR = [(2, 0), (2, 1), (1, 0), (3, 0), (1, 1), (3, 1), (0, 1)]
A_NEAR = A_FAR[::-1]
Z_FAR = [4, 3, 5, 2, 6, 1, 7]


def fold_gram(gram, factor_t):
    w = lax.dot_general(
        gram,
        factor_t.astype(f32),
        (((0,), (0,)), ((), ())),
        precision=lax.Precision.HIGHEST,
        preferred_element_type=f32,
    )
    w1 = w.astype(bf16)
    return w1, (w - w1.astype(f32)).astype(bf16)


def project(w, mat):
    out = lax.dot_general(w, mat, (((1,), (1,)), ((), ())), preferred_element_type=f32)
    return out[0:RANK] + out[RANK : 2 * RANK]


def wide_tiles(chunk):
    return [chunk[h * 16 : h * 16 + 16, j * 128 : j * 128 + 128] for h in range(2) for j in range(2)]


def wide(ref, d):
    return jnp.concatenate(
        [
            jnp.concatenate([ref[d, 0], ref[d, 1]], axis=1),
            jnp.concatenate([ref[d, 2], ref[d, 3]], axis=1),
        ],
        axis=0,
    )


def narrow(ref):
    return jnp.concatenate(
        [jnp.concatenate([ref[4 * h + j, 4] for j in range(4)], axis=1) for h in range(2)], axis=0
    )


def reduce_kernel(
    replicas,
    all_devices,
    gq,
    eq,
    go,
    eo,
    fq,
    fo,
    giq,
    gio,
    nrm,
    mq,
    mo,
    gp_out,
    gn_out,
    norm_out,
    gq_v,
    eq_v,
    go_v,
    eo_v,
    fq_v,
    fo_v,
    giq_v,
    gio_v,
    nrm_v,
    wq,
    wo,
    send_a,
    recv_a,
    zbuf,
    gath,
    nsrc,
    nrecv,
    nz,
    nx,
    ng,
    sem_q,
    sem_o,
    sem_s,
    sem_as,
    sem_ar,
    sem_zs,
    sem_zr,
    sem_gs,
    sem_gr,
    nsem_as,
    nsem_ar,
    nsem_zs,
    nsem_zr,
    nsem_xs,
    nsem_xr,
    nsem_gs,
    nsem_gr,
):
    rep = lax.axis_index("replica")
    ten = lax.axis_index("tensor")
    nx_size = lax.axis_size("tensor")
    y = rep // (NZ * NC)
    z = (rep // NC) % NZ
    core = rep % NC
    a = y * NC + core

    def a_peer(off):
        py, pc = (y + off[0]) % NY, (core + off[1]) % NC
        return py * NC + pc, ((py * NZ + z) * NC + pc, ten)

    def z_peer(dz):
        pz = (z + dz) % NZ
        return pz, ((y * NZ + pz) * NC + core, ten)

    def x_peer(dx):
        px = (ten + dx) % nx_size
        return px, (rep, px)

    small = [(fo, fo_v), (gio, gio_v), (fq, fq_v), (giq, giq_v), (nrm, nrm_v)]
    small_copies = [pltpu.make_async_copy(s, d, sem_s.at[i]) for i, (s, d) in enumerate(small)]
    for c in small_copies:
        c.start()
    o_rows = go.shape[0] // 4
    q_rows = gq.shape[0] // NA

    def o_loads(j):
        rows = pl.ds(j * o_rows, o_rows)
        return [
            pltpu.make_async_copy(go.at[rows, :], go_v.at[rows, :], sem_o.at[0, j]),
            pltpu.make_async_copy(eo.at[rows, :], eo_v.at[rows, :], sem_o.at[1, j]),
        ]

    def q_slice(d):
        return pl.ds(pl.multiple_of(d * q_rows, q_rows), q_rows)

    def q_loads(d):
        rows = q_slice(d)
        return [
            pltpu.make_async_copy(gq.at[rows, :], gq_v.at[rows, :], sem_q.at[0, d]),
            pltpu.make_async_copy(eq.at[rows, :], eq_v.at[rows, :], sem_q.at[1, d]),
        ]

    order = A_FAR + [(0, 0)]
    for j in range(4):
        for c in o_loads(j):
            c.start()
    for off in order:
        for c in q_loads(a_peer(off)[0]):
            c.start()

    barrier = pltpu.get_barrier_semaphore()
    for off in A_FAR:
        pl.semaphore_signal(barrier, inc=1, device_id=a_peer(off)[1], device_id_type=MESH)
    for dz in Z_FAR:
        pl.semaphore_signal(barrier, inc=1, device_id=z_peer(dz)[1], device_id_type=MESH)
    for dx in range(1, nx_size):
        pl.semaphore_signal(barrier, inc=1, device_id=x_peer(dx)[1], device_id_type=MESH)

    def exchange(src, dst, send_sem, recv_sem, device):
        return pltpu.make_async_remote_copy(
            src_ref=src, dst_ref=dst, send_sem=send_sem, recv_sem=recv_sem,
            device_id=device, device_id_type=MESH,
        )

    def a_copy(ph, off):
        d, dev = a_peer(off)
        return exchange(send_a.at[ph, d], recv_a.at[ph, a], sem_as.at[ph, d], sem_ar.at[ph, a], dev)

    def a_wait(ph, off):
        d, dev = a_peer(off)
        exchange(send_a.at[ph, d], recv_a.at[ph, d], sem_as.at[ph, d], sem_ar.at[ph, d], dev).wait_recv()
        return recv_a[ph, d].astype(f32)

    def z_copy(ph, dz):
        d, dev = z_peer(dz)
        return exchange(zbuf.at[ph, z], zbuf.at[ph, z], sem_zs.at[ph, d], sem_zr.at[ph, z], dev)

    def z_wait(ph, dz):
        d, dev = z_peer(dz)
        exchange(zbuf.at[ph, d], zbuf.at[ph, d], sem_zs.at[ph, d], sem_zr.at[ph, d], dev).wait_recv()

    def g_copy(ph, off):
        d, dev = a_peer(off)
        return exchange(gath.at[ph, a], gath.at[ph, a], sem_gs.at[ph, d], sem_gr.at[ph, a], dev)

    def g_wait(ph, off):
        d, dev = a_peer(off)
        exchange(gath.at[ph, d], gath.at[ph, d], sem_gs.at[ph, d], sem_gr.at[ph, d], dev).wait_recv()
        return d

    def na_copy(off):
        d, dev = a_peer(off)
        return exchange(nsrc.at[d], nrecv.at[a], nsem_as.at[d], nsem_ar.at[a], dev)

    def na_wait(off):
        d, dev = a_peer(off)
        exchange(nsrc.at[d], nrecv.at[d], nsem_as.at[d], nsem_ar.at[d], dev).wait_recv()
        return nrecv[d]

    def nz_copy(dz):
        d, dev = z_peer(dz)
        return exchange(nz.at[z], nz.at[z], nsem_zs.at[d], nsem_zr.at[z], dev)

    def nz_wait(dz):
        d, dev = z_peer(dz)
        exchange(nz.at[d], nz.at[d], nsem_zs.at[d], nsem_zr.at[d], dev).wait_recv()

    def nx_copy(dx):
        d, dev = x_peer(dx)
        return exchange(nx.at[ten], nx.at[ten], nsem_xs.at[d], nsem_xr.at[ten], dev)

    def nx_wait(dx):
        d, dev = x_peer(dx)
        exchange(nx.at[d], nx.at[d], nsem_xs.at[d], nsem_xr.at[d], dev).wait_recv()

    def ng_copy(off):
        d, dev = a_peer(off)
        return exchange(ng.at[a], ng.at[a], nsem_gs.at[d], nsem_gr.at[a], dev)

    def ng_wait(off):
        d, dev = a_peer(off)
        exchange(ng.at[d], ng.at[d], nsem_gs.at[d], nsem_gr.at[d], dev).wait_recv()

    small_copies[0].wait()
    small_copies[1].wait()
    for i, w in enumerate(fold_gram(gio_v[...], fo_v[...])):
        wo[i * RANK : (i + 1) * RANK, :] = w
    small_copies[2].wait()
    small_copies[3].wait()
    for i, w in enumerate(fold_gram(giq_v[...], fq_v[...])):
        wq[i * RANK : (i + 1) * RANK, :] = w
    for j in range(4):
        for c in o_loads(j):
            c.wait()
        rows = pl.ds(j * o_rows, o_rows)
        mat = go_v[rows, :] + eo_v[rows, :]
        mo[rows, :] = mat
        part = project(wo[...], mat).astype(bf16)
        send_a[0, j, 4] = part[0:16]
        send_a[0, 4 + j, 4] = part[16:32]

    n_others = len(A_FAR) + len(Z_FAR) + nx_size - 1
    for i, off in enumerate(order):
        d, _ = a_peer(off)
        for c in q_loads(d):
            c.wait()
        rows = q_slice(d)
        mat = gq_v[rows, :] + eq_v[rows, :]
        mq[rows, :] = mat
        part = project(wq[...], mat).astype(bf16)
        for t, tile in enumerate(wide_tiles(part)):
            send_a[0, d, t] = tile
        if i == 0:
            pl.semaphore_wait(barrier, n_others)
        if off != (0, 0):
            a_copy(0, off).start()

    small_copies[4].wait()
    piece = nsrc.shape[2]
    for d in range(NA):
        nsrc[d] = nrm_v[0, :, d * piece : (d + 1) * piece].astype(f32)
    for off in A_FAR:
        na_copy(off).start()

    def sum_a(ph):
        total = send_a[ph, a].astype(f32)
        for off in A_NEAR:
            total = total + a_wait(ph, off)
        zbuf[ph, z] = total.astype(bf16)
        for dz in Z_FAR:
            z_copy(ph, dz).start()

    def sum_z(ph, divisor):
        for dz in Z_FAR[::-1]:
            z_wait(ph, dz)
        total = zbuf[ph, 0].astype(f32)
        for k in range(1, NZ):
            total = total + zbuf[ph, k].astype(f32)
        if divisor is not None:
            total = total / divisor
        gath[ph, a] = total.astype(bf16)
        for off in A_FAR:
            g_copy(ph, off).start()

    sum_a(0)

    ntotal = nsrc[a]
    for off in A_NEAR:
        ntotal = ntotal + na_wait(off)
    nz[z] = ntotal
    for dz in Z_FAR:
        nz_copy(dz).start()
    for off in A_FAR:
        a_copy(0, off).wait_send()

    sum_z(0, None)

    for dz in Z_FAR:
        nz_wait(dz)
    ntotal = nz[0]
    for k in range(1, NZ):
        ntotal = ntotal + nz[k]
    nx[ten] = ntotal
    for dx in range(1, nx_size):
        nx_copy(dx).start()
    for dz in Z_FAR:
        z_copy(0, dz).wait_send()
        nz_copy(dz).wait_send()
    for off in A_FAR:
        na_copy(off).wait_send()

    acc_q = jnp.zeros((RANK, mq.shape[1]), f32)
    for group in ([(0, 0)] + A_NEAR[:5], A_NEAR[5:]):
        for off in group:
            if off != (0, 0):
                g_wait(0, off)
        for off in group:
            d = a_peer(off)[0]
            acc_q = acc_q + jnp.dot(wide(gath.at[0], d), mq[q_slice(d), :], preferred_element_type=f32)
    left = narrow(gath.at[0])
    o_cols = mo.shape[1] // NA
    for d in range(NA):
        part = jnp.dot(left, mo[:, d * o_cols : (d + 1) * o_cols], preferred_element_type=f32).astype(bf16)
        for t, tile in enumerate(wide_tiles(part)):
            send_a[1, d, t] = tile
        h, j = d // 4, d % 4
        send_a[1, d, 4] = acc_q[h * 16 : h * 16 + 16, j * 128 : j * 128 + 128].astype(bf16)
    for off in A_FAR:
        a_copy(1, off).start()

    gp_out[...] = gath[0]
    for dx in range(1, nx_size):
        nx_wait(dx)
    ntotal = nx[0]
    for k in range(1, nx_size):
        ntotal = ntotal + nx[k]
    ng[a] = ntotal / all_devices
    for off in A_FAR:
        ng_copy(off).start()
    for off in A_FAR:
        g_copy(0, off).wait_send()
    for dx in range(1, nx_size):
        nx_copy(dx).wait_send()

    sum_a(1)

    for off in A_FAR:
        ng_wait(off)
    for d in range(NA):
        norm_out[:, d * piece : (d + 1) * piece] = ng[d]
    for off in A_FAR:
        a_copy(1, off).wait_send()
        ng_copy(off).wait_send()

    sum_z(1, replicas)

    for dz in Z_FAR:
        z_copy(1, dz).wait_send()
    for off in A_NEAR:
        g_wait(1, off)
    gn_out[...] = gath[1]
    for off in A_FAR:
        g_copy(1, off).wait_send()


def outer(left_t, right_t):
    return lax.dot_general(left_t, right_t, (((0,), (0,)), ((), ())), preferred_element_type=f32)


def update_kernel(
    gp, gn, nrm, mq, mo, wq, mom_q, wo, mom_o,
    eq_out, eo_out, fq_out, fo_out, momq_out, wq_out, momo_out, wo_out, norm_out,
    eq_v, eo_v, fq_v, fo_v, small_v, turn, sem_q, sem_o, sem_s,
):
    rep = lax.axis_index("replica")
    copies = []

    def put(src, dst, sem):
        c = pltpu.make_async_copy(src, dst, sem)
        c.start()
        copies.append(c)

    put(nrm, norm_out, sem_s.at[0])
    right_q = narrow(gn)
    left_o = narrow(gp)
    q_rows, o_cols = mq.shape[0] // NA, mo.shape[1] // NA
    for d in range(NA):
        rows = slice(d * q_rows, (d + 1) * q_rows)
        approx = outer(wide(gp, d), right_q)
        eq_v[rows, :] = (mq[rows, :].astype(f32) - approx).astype(bf16)
        put(eq_v.at[pl.ds(d * q_rows, q_rows), :], eq_out.at[pl.ds(d * q_rows, q_rows), :], sem_q.at[d])
    o_rows = mo.shape[0] // 4
    for d in range(NA):
        fo_v[:, d * o_cols : (d + 1) * o_cols] = wide(gn, d)
    fq_v[...] = right_q
    put(fq_v, fq_out, sem_s.at[1])
    put(fo_v, fo_out, sem_s.at[2])
    for j in range(4):
        rows = slice(j * o_rows, (j + 1) * o_rows)
        approx = outer(left_o[:, rows], fo_v[...])
        eo_v[rows, :] = (mo[rows, :].astype(f32) - approx).astype(bf16)
        put(eo_v.at[pl.ds(j * o_rows, o_rows), :], eo_out.at[pl.ds(j * o_rows, o_rows), :], sem_o.at[j])
    c = rep // 8
    off = pl.multiple_of((rep % 8) * RANK, RANK)
    turn[0] = wide(gp, c).astype(f32).T
    turn[1] = wide(gn, c).astype(f32).T
    for k, (right, mom, w) in enumerate([(right_q, mom_q, wq), (left_o, mom_o, wo)]):
        left = turn[k, pl.ds(off, RANK), :].astype(bf16)
        m = momentum_decay * mom[...] + jnp.dot(left, right, preferred_element_type=f32)
        small_v[2 * k] = m
        small_v[2 * k + 1] = w[...] - step_size * m
    for k, out in enumerate([momq_out, wq_out, momo_out, wo_out]):
        put(small_v.at[k], out, sem_s.at[3 + k])
    for c in copies:
        c.wait()


def on_device(
    grad_q,
    error_q,
    qfac_q,
    ginv_q,
    weight_q,
    momentum_q,
    grad_o,
    error_o,
    qfac_o,
    ginv_o,
    weight_o,
    momentum_o,
    norm_grads,
):
    replicas = lax.axis_size("replica")
    tensors = lax.axis_size("tensor")
    shape_q, shape_o = grad_q.shape, grad_o.shape
    piece = norm_grads.shape[2] // NA
    packed = (NA, TILES, 16, 128)
    hbm = pl.BlockSpec(memory_space=pltpu.HBM)
    vmem = pl.BlockSpec(memory_space=pltpu.VMEM)
    dma = pltpu.SemaphoreType.DMA
    mat_q, mat_o, gp, gn, norm = pl.pallas_call(
        functools.partial(reduce_kernel, replicas, replicas * tensors),
        out_shape=(
            pltpu.VMEM(shape_q, bf16),
            pltpu.VMEM(shape_o, bf16),
            pltpu.VMEM(packed, bf16),
            pltpu.VMEM(packed, bf16),
            pltpu.VMEM((1, NA * piece), f32),
        ),
        in_specs=[hbm] * 9,
        out_specs=(vmem,) * 5,
        scratch_shapes=[
            pltpu.VMEM(shape_q, bf16),
            pltpu.VMEM(shape_q, bf16),
            pltpu.VMEM(shape_o, bf16),
            pltpu.VMEM(shape_o, bf16),
            pltpu.VMEM((RANK, shape_q[1]), bf16),
            pltpu.VMEM((RANK, shape_o[1]), bf16),
            pltpu.VMEM((RANK, RANK), f32),
            pltpu.VMEM((RANK, RANK), f32),
            pltpu.VMEM(norm_grads.shape, bf16),
            pltpu.VMEM((2 * RANK, shape_q[1]), bf16),
            pltpu.VMEM((2 * RANK, shape_o[1]), bf16),
            pltpu.VMEM((2,) + packed, bf16),
            pltpu.VMEM((2,) + packed, bf16),
            pltpu.VMEM((2,) + packed, bf16),
            pltpu.VMEM((2,) + packed, bf16),
            pltpu.VMEM((NA, 1, piece), f32),
            pltpu.VMEM((NA, 1, piece), f32),
            pltpu.VMEM((NZ, 1, piece), f32),
            pltpu.VMEM((tensors, 1, piece), f32),
            pltpu.VMEM((NA, 1, piece), f32),
            dma((2, NA)),
            dma((2, 4)),
            dma((5,)),
            dma((2, NA)),
            dma((2, NA)),
            dma((2, NZ)),
            dma((2, NZ)),
            dma((2, NA)),
            dma((2, NA)),
            dma((NA,)),
            dma((NA,)),
            dma((NZ,)),
            dma((NZ,)),
            dma((tensors,)),
            dma((tensors,)),
            dma((NA,)),
            dma((NA,)),
        ],
        compiler_params=pltpu.CompilerParams(
            collective_id=0, has_side_effects=True, vmem_limit_bytes=24 << 20
        ),
        name="reduce_factors",
    )(
        *(
            pltpu.with_memory_space_constraint(x, pltpu.HBM)
            for x in (grad_q, error_q, grad_o, error_o, qfac_q.T, qfac_o.T, ginv_q, ginv_o, norm_grads)
        )
    )

    wide_piece = (RANK, shape_q[1])
    outs = pl.pallas_call(
        update_kernel,
        out_shape=(
            jax.ShapeDtypeStruct(shape_q, bf16),
            jax.ShapeDtypeStruct(shape_o, bf16),
            jax.ShapeDtypeStruct((RANK, shape_q[1]), bf16),
            jax.ShapeDtypeStruct((RANK, shape_o[1]), bf16),
            jax.ShapeDtypeStruct(wide_piece, f32),
            jax.ShapeDtypeStruct(wide_piece, f32),
            jax.ShapeDtypeStruct(wide_piece, f32),
            jax.ShapeDtypeStruct(wide_piece, f32),
            jax.ShapeDtypeStruct((1, NA * piece), f32),
        ),
        in_specs=[vmem] * 9,
        out_specs=(hbm,) * 9,
        scratch_shapes=[
            pltpu.VMEM(shape_q, bf16),
            pltpu.VMEM(shape_o, bf16),
            pltpu.VMEM((RANK, shape_q[1]), bf16),
            pltpu.VMEM((RANK, shape_o[1]), bf16),
            pltpu.VMEM((4,) + wide_piece, f32),
            pltpu.VMEM((2, 256, RANK), f32),
            dma((NA,)),
            dma((4,)),
            dma((7,)),
        ],
        compiler_params=pltpu.CompilerParams(vmem_limit_bytes=16 << 20),
        name="apply_update",
    )(gp, gn, norm, mat_q, mat_o, weight_q, momentum_q, weight_o.T, momentum_o.T)
    error_q_new, error_o_new, fq_t, fo_t, momq, wq, momo_t, wo_t, norm_mean = outs
    return (
        error_q_new,
        fq_t.T,
        momq,
        wq,
        error_o_new,
        fo_t.T,
        momo_t.T,
        wo_t.T,
        norm_mean.reshape(-1),
    )


def solution(mesh):
    in_specs = (
        P("replica", "tensor"),
        P("replica", "tensor"),
        P("tensor", None),
        P("tensor", None),
        P("replica", "tensor"),
        P("replica", "tensor"),
        P(("replica", "tensor"), None),
        P(("replica", "tensor"), None),
        P("tensor", None),
        P("tensor", None),
        P("tensor", "replica"),
        P("tensor", "replica"),
        P("replica", "tensor", None),
    )
    out_specs = (
        P("replica", "tensor"),
        P("tensor", None),
        P("replica", "tensor"),
        P("replica", "tensor"),
        P(("replica", "tensor"), None),
        P("tensor", None),
        P("tensor", "replica"),
        P("tensor", "replica"),
        P(),
    )
    return jax.shard_map(
        on_device, mesh=mesh, in_specs=in_specs, out_specs=out_specs, check_vma=False
    )
```

time: 50.8 us -> 45.8 us (0.902)
  Pallas kernels: 50 us -> 45 us
    pallas_call x1, Pallas kernels: 5.81 us -> 2.57 us  [on_device(): pl.pallas_call(update_kernel, out_shape=(jax.ShapeDtypeStruct(shape_q, bf...]
    pallas_call x1, Pallas kernels: 44.2 us -> 42.4 us  [on_device(): pl.pallas_call(functools.partial(reduce_kernel, replicas, replicas * tens...]
where the time goes in v2:
time: 45.8 us; the launch traced here: 45.7 us
  Pallas kernels  45 us (98%)
  between operations  0.72 us (2%)
    pallas_call x1, Pallas kernels, on_device(): pl.pallas_call(functools.partial(reduce_kernel, replicas, replicas * tens...  42.4 us
    pallas_call x1, Pallas kernels, on_device(): pl.pallas_call(update_kernel, out_shape=(jax.ShapeDtypeStruct(shape_q, bf...  2.57 us

profile of v2, /device:TPU:1, one launch (start us, length us, event | category | flops | bytes accessed | tf_op | source)
XLA Modules:
  0.0 45.7 jit_solution(3064897187620770194)
XLA Ops:
  0.6 0.0 copy-start
  0.7 0.0 copy-start.1
  0.7 0.0 copy-start.2
  0.7 0.0 copy-start.3
  0.7 42.4 %reduce_factors.1 = (bf16[2048,512]{1,0:T(8,128)(2,1)S(1)}, bf16[512,2048]{1,0:T(8,128)(2,1)S(1)}, bf16[8,5,16,128]{3,2,1,0:T(8,128)(2,1)S(1)}, bf16[8,5,16,128]{3,2,1,0:T(8,128)(2,1)S(1)}, f32[1,4096]{1,0:T(1,128)S(1)}) custom-call(bf16[2048,512]{1,0:T(8,128)(2,1)} %gq.1, bf16[2048,512]{1,0:T(8,128)(2,1)} %eq.1, bf16[512,2048]{1,0:T(8,128)(2,1)} %go.1, ...), custom_call_target="tpu_custom_call" | custom-call | tf_op jit(solution)/shard_map/reduce_factors/pallas_call | solution.py:460
  43.1 0.0 copy-done
  43.1 0.0 copy-done.1
  43.1 0.0 copy-done.2
  43.1 0.0 copy-done.3
  43.1 2.6 %apply_update.1 = (bf16[2048,512]{1,0:T(8,128)(2,1)}, bf16[512,2048]{1,0:T(8,128)(2,1)}, bf16[32,512]{1,0:T(8,128)(2,1)}, bf16[32,2048]{1,0:T(8,128)(2,1)}, f32[...) custom-call(bf16[8,5,16,128]{3,2,1,0:T(8,128)(2,1)S(1)} %get-tuple-element., ...), custom_call_target="tpu_custom_call" | custom-call | tf_op jit(solution)/shard_map/apply_update/pallas_call | solution.py:522
Async XLA Ops:
  0.6 42.5 %copy-start = (f32[32,512]{1,0:T(8,128)S(1)}, f32[32,512]{1,0:T(8,128)}, u32[]{:S(2)}) copy-start(f32[32,512]{1,0:T(8,128)} %wq.1) | copy-start | bytes 196612
  0.7 42.5 %copy-start.1 = (f32[32,512]{1,0:T(8,128)S(1)}, f32[32,512]{1,0:T(8,128)}, u32[]{:S(2)}) copy-start(f32[32,512]{1,0:T(8,128)} %mom_q.1) | copy-start | bytes 196612
  0.7 42.5 %copy-start.2 = (f32[512,32]{0,1:T(8,128)S(1)}, f32[512,32]{0,1:T(8,128)}, u32[]{:S(2)}) copy-start(f32[512,32]{0,1:T(8,128)} %param.23) | copy-start | bytes 196612
  0.7 42.5 %copy-start.3 = (f32[512,32]{0,1:T(8,128)S(1)}, f32[512,32]{0,1:T(8,128)}, u32[]{:S(2)}) copy-start(f32[512,32]{0,1:T(8,128)} %param.24) | copy-start | bytes 196612

commit v3 on v2

v3 whole, which is shorter than its diff:
```python
import functools

import jax
import jax.numpy as jnp
from jax import lax
from jax.experimental import pallas as pl
from jax.experimental.pallas import tpu as pltpu
from jax.sharding import PartitionSpec as P

momentum_decay = 0.9
step_size = 0.5

NY, NZ, NC = 4, 8, 2
NA = NY * NC
RANK = 32
TILES = 5
MESH = pl.DeviceIdType.MESH
f32 = jnp.float32
bf16 = jnp.bfloat16

A_FAR = [(2, 0), (2, 1), (1, 0), (3, 0), (1, 1), (3, 1), (0, 1)]
A_NEAR = A_FAR[::-1]
Z_FAR = [4, 3, 5, 2, 6, 1, 7]
Y_FAR = [2, 1, 3, 0]


def fold_gram(gram, factor_t):
    w = lax.dot_general(
        gram,
        factor_t.astype(f32),
        (((0,), (0,)), ((), ())),
        precision=lax.Precision.HIGHEST,
        preferred_element_type=f32,
    )
    w1 = w.astype(bf16)
    return jnp.concatenate([w1, (w - w1.astype(f32)).astype(bf16)], axis=0)


def project(mat, w):
    out = lax.dot_general(w, mat, (((1,), (1,)), ((), ())), preferred_element_type=f32)
    return (out[0:RANK] + out[RANK : 2 * RANK]).astype(bf16)


def project_nn(mat, w):
    out = jnp.dot(mat, w, preferred_element_type=f32)
    return (out[:, 0:RANK] + out[:, RANK : 2 * RANK]).T.astype(bf16)


def wide_tiles(chunk):
    return [chunk[h * 16 : h * 16 + 16, j * 128 : j * 128 + 128] for h in range(2) for j in range(2)]


def wide(ref, d):
    return jnp.concatenate(
        [
            jnp.concatenate([ref[d, 0], ref[d, 1]], axis=1),
            jnp.concatenate([ref[d, 2], ref[d, 3]], axis=1),
        ],
        axis=0,
    )


def narrow(ref):
    return jnp.concatenate(
        [jnp.concatenate([ref[4 * h + j] for j in range(4)], axis=1) for h in range(2)], axis=0
    )


def reduce_kernel(
    replicas,
    all_devices,
    gq,
    eq,
    go,
    eo,
    fq,
    fo,
    giq,
    gio,
    nrm,
    mq,
    mo,
    gp_out,
    gn_out,
    norm_out,
    q_v,
    o_v,
    fq_v,
    fo_v,
    giq_v,
    gio_v,
    nrm_v,
    wq,
    wo,
    sa0,
    sa1,
    ra0,
    ra1,
    zb0,
    zb1,
    ga0,
    ga1,
    nsrc,
    nrecv,
    nz,
    nx,
    ng,
    sem_l,
    sem_s,
    sem_as,
    sem_ar,
    sem_zs,
    sem_zr,
    sem_gs,
    sem_gr,
    nsem_s,
    nsem_r,
):
    rep = lax.axis_index("replica")
    ten = lax.axis_index("tensor")
    nx_size = lax.axis_size("tensor")
    y = rep // (NZ * NC)
    z = (rep // NC) % NZ
    core = rep % NC
    a = y * NC + core

    def a_peer(off):
        py, pc = (y + off[0]) % NY, (core + off[1]) % NC
        return py * NC + pc, ((py * NZ + z) * NC + pc, ten)

    def z_peer(dz):
        pz = (z + dz) % NZ
        return pz, ((y * NZ + pz) * NC + core, ten)

    def x_peer(dx):
        px = (ten + dx) % nx_size
        return px, (rep, px)

    small = [(fo, fo_v), (gio, gio_v), (fq, fq_v), (giq, giq_v), (nrm, nrm_v)]
    small_copies = [pltpu.make_async_copy(s, d, sem_s.at[i]) for i, (s, d) in enumerate(small)]
    for c in small_copies:
        c.start()
    o_rows = go.shape[0] // 2
    q_rows = gq.shape[0] // NY

    def block(i):
        if i < 2:
            return go, eo, o_v, pl.ds(i * o_rows, o_rows)
        at = ((y + Y_FAR[i - 2]) % NY) * q_rows
        return gq, eq, q_v, pl.ds(pl.multiple_of(at, q_rows), q_rows)

    for i in range(2 + NY):
        g, e, v, rows = block(i)
        pltpu.make_async_copy(g.at[rows, :], v.at[0, rows, :], sem_l.at[i]).start()
        pltpu.make_async_copy(e.at[rows, :], v.at[1, rows, :], sem_l.at[i]).start()

    def load_sum(i, out):
        _, _, v, rows = block(i)
        both = v.at[:, rows, :]
        pltpu.make_async_copy(both, both, sem_l.at[i]).wait()
        out[rows, :] = v[0, rows, :] + v[1, rows, :]
        return rows

    barrier = pltpu.get_barrier_semaphore()
    for off in A_FAR:
        pl.semaphore_signal(barrier, inc=1, device_id=a_peer(off)[1], device_id_type=MESH)
    for dz in Z_FAR:
        pl.semaphore_signal(barrier, inc=1, device_id=z_peer(dz)[1], device_id_type=MESH)
    for dx in range(1, nx_size):
        pl.semaphore_signal(barrier, inc=1, device_id=x_peer(dx)[1], device_id_type=MESH)

    def exchange(src, dst, send_sem, recv_sem, device):
        return pltpu.make_async_remote_copy(
            src_ref=src, dst_ref=dst, send_sem=send_sem, recv_sem=recv_sem,
            device_id=device, device_id_type=MESH,
        )

    def part_of(ref, ph, d, kind):
        return ref[kind].at[ph, d]

    def wait_seven(ref, ph, kind, sem):
        seven = ref[kind].at[ph, pl.ds(0, NA - 1)]
        pltpu.make_async_copy(seven, seven, sem.at[ph, kind]).wait()

    send_a, recv_a, zbuf, gath = (sa0, sa1), (ra0, ra1), (zb0, zb1), (ga0, ga1)

    def a_send(ph, kind, offs):
        for off in offs:
            d, dev = a_peer(off)
            exchange(
                part_of(send_a, ph, d, kind), part_of(recv_a, ph, a, kind),
                sem_as.at[ph, kind], sem_ar.at[ph, kind], dev,
            ).start()

    def z_send(ph, kind):
        mine = part_of(zbuf, ph, z, kind)
        for dz in Z_FAR:
            exchange(mine, mine, sem_zs.at[ph, kind], sem_zr.at[ph, kind], z_peer(dz)[1]).start()

    def g_send(ph, kind):
        mine = part_of(gath, ph, a, kind)
        for off in A_FAR:
            exchange(mine, mine, sem_gs.at[ph, kind], sem_gr.at[ph, kind], a_peer(off)[1]).start()

    def norm_wait(ref, n, sem):
        some = ref.at[pl.ds(0, n)]
        pltpu.make_async_copy(some, some, sem).wait()

    def norm_send(src, dst, step, devices):
        for dev in devices:
            exchange(src, dst, nsem_s.at[step], nsem_r.at[step], dev).start()

    a_devices = [a_peer(off)[1] for off in A_FAR]
    z_devices = [z_peer(dz)[1] for dz in Z_FAR]
    x_devices = [x_peer(dx)[1] for dx in range(1, nx_size)]

    small_copies[0].wait()
    small_copies[1].wait()
    wo[...] = fold_gram(gio_v[...], fo_v[...]).T
    small_copies[2].wait()
    small_copies[3].wait()
    wq[...] = fold_gram(giq_v[...], fq_v[...])
    for i in range(2):
        part = project_nn(mo[load_sum(i, mo), :], wo[...])
        for j in range(2):
            for h in range(2):
                sa1[0, 4 * h + 2 * i + j] = part[16 * h : 16 * h + 16, 128 * j : 128 * j + 128]

    n_others = len(A_FAR) + len(Z_FAR) + nx_size - 1
    pl.semaphore_wait(barrier, n_others)
    a_send(0, 1, A_FAR)

    for i in range(NY):
        part = project(mq[load_sum(2 + i, mq), :], wq[...])
        for c in range(NC):
            d = ((y + Y_FAR[i]) % NY) * NC + c
            for t, tile in enumerate(wide_tiles(part[:, 256 * c : 256 * c + 256])):
                sa0[0, d, t] = tile
        a_send(0, 0, [off for off in A_FAR if off[0] == Y_FAR[i]])

    def sum_a(ph, kind):
        wait_seven(recv_a, ph, kind, sem_ar)
        total = part_of(send_a, ph, a, kind)[...].astype(f32)
        for off in A_NEAR:
            total = total + part_of(recv_a, ph, a_peer(off)[0], kind)[...].astype(f32)
        part_of(zbuf, ph, z, kind)[...] = total.astype(bf16)
        z_send(ph, kind)

    def sum_z(ph, kind, divisor):
        wait_seven(zbuf, ph, kind, sem_zr)
        total = part_of(zbuf, ph, 0, kind)[...].astype(f32)
        for k in range(1, NZ):
            total = total + part_of(zbuf, ph, k, kind)[...].astype(f32)
        if divisor is not None:
            total = total / divisor
        part_of(gath, ph, a, kind)[...] = total.astype(bf16)
        g_send(ph, kind)

    def sent(ph, kind):
        wait_seven(send_a, ph, kind, sem_as)
        wait_seven(zbuf, ph, kind, sem_zs)

    small_copies[4].wait()
    piece = nsrc.shape[2]
    for d in range(NA):
        nsrc[d] = nrm_v[0, :, d * piece : (d + 1) * piece].astype(f32)
    for off in A_FAR:
        d, dev = a_peer(off)
        norm_send(nsrc.at[d], nrecv.at[a], 0, [dev])

    sum_a(0, 1)
    sum_a(0, 0)

    norm_wait(nrecv, NA - 1, nsem_r.at[0])
    ntotal = nsrc[a]
    for off in A_NEAR:
        ntotal = ntotal + nrecv[a_peer(off)[0]]
    nz[z] = ntotal
    norm_send(nz.at[z], nz.at[z], 1, z_devices)

    sum_z(0, 1, None)

    wait_seven(gath, 0, 1, sem_gr)
    left = narrow(ga1.at[0])
    o_cols = mo.shape[1] // NA
    for d in range(NA):
        part = jnp.dot(left, mo[:, d * o_cols : (d + 1) * o_cols], preferred_element_type=f32).astype(bf16)
        for t, tile in enumerate(wide_tiles(part)):
            sa0[1, d, t] = tile
    a_send(1, 0, A_FAR)

    sum_z(0, 0, None)

    norm_wait(nz, NZ - 1, nsem_r.at[1])
    ntotal = nz[0]
    for k in range(1, NZ):
        ntotal = ntotal + nz[k]
    nx[ten] = ntotal
    norm_send(nx.at[ten], nx.at[ten], 2, x_devices)

    sum_a(1, 0)

    chunk = mq.shape[0] // NA
    wait_seven(gath, 0, 0, sem_gr)
    left = jnp.concatenate([wide(ga0.at[0], d) for d in range(NA)], axis=1)
    acc = jnp.dot(left, mq[...], preferred_element_type=f32).astype(bf16)
    for d in range(NA):
        h, j = d // 4, d % 4
        sa1[1, d] = acc[h * 16 : h * 16 + 16, j * 128 : j * 128 + 128]
    a_send(1, 1, A_FAR)

    gp_out[:, 0:4] = ga0[0]
    gp_out[:, 4] = ga1[0]
    norm_wait(nx, nx_size - 1, nsem_r.at[2])
    ntotal = nx[0]
    for k in range(1, nx_size):
        ntotal = ntotal + nx[k]
    ng[a] = ntotal / all_devices
    norm_send(ng.at[a], ng.at[a], 3, a_devices)
    norm_wait(nsrc, NA - 1, nsem_s.at[0])
    norm_wait(nz, NZ - 1, nsem_s.at[1])
    norm_wait(nx, nx_size - 1, nsem_s.at[2])

    sum_a(1, 1)
    sum_z(1, 0, replicas)

    norm_wait(ng, NA - 1, nsem_r.at[3])
    for d in range(NA):
        norm_out[:, d * piece : (d + 1) * piece] = ng[d]
    norm_wait(ng, NA - 1, nsem_s.at[3])
    for kind in range(2):
        sent(0, kind)
        wait_seven(gath, 0, kind, sem_gs)
    sent(1, 0)

    sum_z(1, 1, replicas)

    wait_seven(gath, 1, 0, sem_gr)
    gn_out[:, 0:4] = ga0[1]
    wait_seven(gath, 1, 0, sem_gs)
    sent(1, 1)
    wait_seven(gath, 1, 1, sem_gr)
    gn_out[:, 4] = ga1[1]
    wait_seven(gath, 1, 1, sem_gs)


def outer(left_t, right_t):
    return lax.dot_general(left_t, right_t, (((0,), (0,)), ((), ())), preferred_element_type=f32)


def update_kernel(
    gp, gn, nrm, mq, mo, wq, mom_q, wo, mom_o,
    eq_out, eo_out, fq_out, fo_out, momq_out, wq_out, momo_out, wo_out, norm_out,
    eq_v, eo_v, fq_v, fo_v, small_v, turn, sem_q, sem_o, sem_s,
):
    rep = lax.axis_index("replica")
    copies = []

    def put(src, dst, sem):
        c = pltpu.make_async_copy(src, dst, sem)
        c.start()
        copies.append(c)

    put(nrm, norm_out, sem_s.at[0])
    right_q = narrow(gn.at[:, 4])
    left_o = narrow(gp.at[:, 4])
    q_rows, o_cols = mq.shape[0] // NA, mo.shape[1] // NA
    for d in range(NA):
        rows = slice(d * q_rows, (d + 1) * q_rows)
        approx = outer(wide(gp, d), right_q)
        eq_v[rows, :] = (mq[rows, :].astype(f32) - approx).astype(bf16)
        put(eq_v.at[pl.ds(d * q_rows, q_rows), :], eq_out.at[pl.ds(d * q_rows, q_rows), :], sem_q.at[d])
    o_rows = mo.shape[0] // 4
    for d in range(NA):
        fo_v[:, d * o_cols : (d + 1) * o_cols] = wide(gn, d)
    fq_v[...] = right_q
    put(fq_v, fq_out, sem_s.at[1])
    put(fo_v, fo_out, sem_s.at[2])
    for j in range(4):
        rows = slice(j * o_rows, (j + 1) * o_rows)
        approx = outer(left_o[:, rows], fo_v[...])
        eo_v[rows, :] = (mo[rows, :].astype(f32) - approx).astype(bf16)
        put(eo_v.at[pl.ds(j * o_rows, o_rows), :], eo_out.at[pl.ds(j * o_rows, o_rows), :], sem_o.at[j])
    c = rep // 8
    off = pl.multiple_of((rep % 8) * RANK, RANK)
    turn[0] = wide(gp, c).astype(f32).T
    turn[1] = wide(gn, c).astype(f32).T
    for k, (right, mom, w) in enumerate([(right_q, mom_q, wq), (left_o, mom_o, wo)]):
        left = turn[k, pl.ds(off, RANK), :].astype(bf16)
        m = momentum_decay * mom[...] + jnp.dot(left, right, preferred_element_type=f32)
        small_v[2 * k] = m
        small_v[2 * k + 1] = w[...] - step_size * m
    for k, out in enumerate([momq_out, wq_out, momo_out, wo_out]):
        put(small_v.at[k], out, sem_s.at[3 + k])
    for c in copies:
        c.wait()


def on_device(
    grad_q,
    error_q,
    qfac_q,
    ginv_q,
    weight_q,
    momentum_q,
    grad_o,
    error_o,
    qfac_o,
    ginv_o,
    weight_o,
    momentum_o,
    norm_grads,
):
    replicas = lax.axis_size("replica")
    tensors = lax.axis_size("tensor")
    shape_q, shape_o = grad_q.shape, grad_o.shape
    piece = norm_grads.shape[2] // NA
    packed = (NA, TILES, 16, 128)
    hbm = pl.BlockSpec(memory_space=pltpu.HBM)
    vmem = pl.BlockSpec(memory_space=pltpu.VMEM)
    dma = pltpu.SemaphoreType.DMA
    mat_q, mat_o, gp, gn, norm = pl.pallas_call(
        functools.partial(reduce_kernel, replicas, replicas * tensors),
        out_shape=(
            pltpu.VMEM(shape_q, bf16),
            pltpu.VMEM(shape_o, bf16),
            pltpu.VMEM(packed, bf16),
            pltpu.VMEM(packed, bf16),
            pltpu.VMEM((1, NA * piece), f32),
        ),
        in_specs=[hbm] * 9,
        out_specs=(vmem,) * 5,
        scratch_shapes=[
            pltpu.VMEM((2,) + shape_q, bf16),
            pltpu.VMEM((2,) + shape_o, bf16),
            pltpu.VMEM((RANK, shape_q[1]), bf16),
            pltpu.VMEM((RANK, shape_o[1]), bf16),
            pltpu.VMEM((RANK, RANK), f32),
            pltpu.VMEM((RANK, RANK), f32),
            pltpu.VMEM(norm_grads.shape, bf16),
            pltpu.VMEM((2 * RANK, shape_q[1]), bf16),
            pltpu.VMEM((shape_o[1], 2 * RANK), bf16),
            *[pltpu.VMEM(shape, bf16) for shape in [(2, NA, 4, 16, 128), (2, NA, 16, 128)] * 4],
            pltpu.VMEM((NA, 1, piece), f32),
            pltpu.VMEM((NA, 1, piece), f32),
            pltpu.VMEM((NZ, 1, piece), f32),
            pltpu.VMEM((tensors, 1, piece), f32),
            pltpu.VMEM((NA, 1, piece), f32),
            dma((2 + NY,)),
            dma((5,)),
            *[dma((2, 2))] * 6,
            dma((4,)),
            dma((4,)),
        ],
        compiler_params=pltpu.CompilerParams(
            collective_id=0, has_side_effects=True, vmem_limit_bytes=24 << 20
        ),
        name="reduce_factors",
    )(
        *(
            pltpu.with_memory_space_constraint(x, pltpu.HBM)
            for x in (grad_q, error_q, grad_o, error_o, qfac_q.T, qfac_o.T, ginv_q, ginv_o, norm_grads)
        )
    )

    wide_piece = (RANK, shape_q[1])
    outs = pl.pallas_call(
        update_kernel,
        out_shape=(
            jax.ShapeDtypeStruct(shape_q, bf16),
            jax.ShapeDtypeStruct(shape_o, bf16),
            jax.ShapeDtypeStruct((RANK, shape_q[1]), bf16),
            jax.ShapeDtypeStruct((RANK, shape_o[1]), bf16),
            jax.ShapeDtypeStruct(wide_piece, f32),
            jax.ShapeDtypeStruct(wide_piece, f32),
            jax.ShapeDtypeStruct(wide_piece, f32),
            jax.ShapeDtypeStruct(wide_piece, f32),
            jax.ShapeDtypeStruct((1, NA * piece), f32),
        ),
        in_specs=[vmem] * 9,
        out_specs=(hbm,) * 9,
        scratch_shapes=[
            pltpu.VMEM(shape_q, bf16),
            pltpu.VMEM(shape_o, bf16),
            pltpu.VMEM((RANK, shape_q[1]), bf16),
            pltpu.VMEM((RANK, shape_o[1]), bf16),
            pltpu.VMEM((4,) + wide_piece, f32),
            pltpu.VMEM((2, 256, RANK), f32),
            dma((NA,)),
            dma((4,)),
            dma((7,)),
        ],
        compiler_params=pltpu.CompilerParams(vmem_limit_bytes=16 << 20),
        name="apply_update",
    )(gp, gn, norm, mat_q, mat_o, weight_q, momentum_q, weight_o.T, momentum_o.T)
    error_q_new, error_o_new, fq_t, fo_t, momq, wq, momo_t, wo_t, norm_mean = outs
    return (
        error_q_new,
        fq_t.T,
        momq,
        wq,
        error_o_new,
        fo_t.T,
        momo_t.T,
        wo_t.T,
        norm_mean.reshape(-1),
    )


def solution(mesh):
    in_specs = (
        P("replica", "tensor"),
        P("replica", "tensor"),
        P("tensor", None),
        P("tensor", None),
        P("replica", "tensor"),
        P("replica", "tensor"),
        P(("replica", "tensor"), None),
        P(("replica", "tensor"), None),
        P("tensor", None),
        P("tensor", None),
        P("tensor", "replica"),
        P("tensor", "replica"),
        P("replica", "tensor", None),
    )
    out_specs = (
        P("replica", "tensor"),
        P("tensor", None),
        P("replica", "tensor"),
        P("replica", "tensor"),
        P(("replica", "tensor"), None),
        P("tensor", None),
        P("tensor", "replica"),
        P("tensor", "replica"),
        P(),
    )
    return jax.shard_map(
        on_device, mesh=mesh, in_specs=in_specs, out_specs=out_specs, check_vma=False
    )
```

time: 45.8 us -> 42.6 us (0.930)
  Pallas kernels: 45 us -> 41.8 us
    pallas_call x1, Pallas kernels: 42.4 us -> 39.2 us  [on_device(): pl.pallas_call(functools.partial(reduce_kernel, replicas, replicas * tens...]
where the time goes in v3:
time: 42.6 us; the launch traced here: 42.5 us
  Pallas kernels  41.8 us (98%)
  between operations  0.72 us (2%)
    pallas_call x1, Pallas kernels, on_device(): pl.pallas_call(functools.partial(reduce_kernel, replicas, replicas * tens...  39.2 us
    pallas_call x1, Pallas kernels, on_device(): pl.pallas_call(update_kernel, out_shape=(jax.ShapeDtypeStruct(shape_q, bf...  2.57 us

profile of v3, /device:TPU:1, one launch (start us, length us, event | category | flops | bytes accessed | tf_op | source)
XLA Modules:
  0.0 42.5 jit_solution(18428833622042106286)
XLA Ops:
  0.6 0.0 copy-start
  0.7 0.0 copy-start.1
  0.7 0.0 copy-start.2
  0.7 0.0 copy-start.3
  0.7 39.2 %reduce_factors.1 = (bf16[2048,512]{1,0:T(8,128)(2,1)S(1)}, bf16[512,2048]{1,0:T(8,128)(2,1)S(1)}, bf16[8,5,16,128]{3,2,1,0:T(8,128)(2,1)S(1)}, bf16[8,5,16,128]{3,2,1,0:T(8,128)(2,1)S(1)}, f32[1,4096]{1,0:T(1,128)S(1)}) custom-call(bf16[2048,512]{1,0:T(8,128)(2,1)} %gq.1, bf16[2048,512]{1,0:T(8,128)(2,1)} %eq.1, bf16[512,2048]{1,0:T(8,128)(2,1)} %go.1, ...), custom_call_target="tpu_custom_call" | custom-call | tf_op jit(solution)/shard_map/reduce_factors/pallas_call | solution.py:422
  39.9 0.0 copy-done
  39.9 0.0 copy-done.1
  39.9 0.0 copy-done.2
  39.9 0.0 copy-done.3
  39.9 2.6 %apply_update.1 = (bf16[2048,512]{1,0:T(8,128)(2,1)}, bf16[512,2048]{1,0:T(8,128)(2,1)}, bf16[32,512]{1,0:T(8,128)(2,1)}, bf16[32,2048]{1,0:T(8,128)(2,1)}, f32[...) custom-call(bf16[8,5,16,128]{3,2,1,0:T(8,128)(2,1)S(1)} %get-tuple-element., ...), custom_call_target="tpu_custom_call" | custom-call | tf_op jit(solution)/shard_map/apply_update/pallas_call | solution.py:467
Async XLA Ops:
  0.6 39.2 %copy-start = (f32[32,512]{1,0:T(8,128)S(1)}, f32[32,512]{1,0:T(8,128)}, u32[]{:S(2)}) copy-start(f32[32,512]{1,0:T(8,128)} %wq.1) | copy-start | bytes 196612
  0.7 39.2 %copy-start.1 = (f32[32,512]{1,0:T(8,128)S(1)}, f32[32,512]{1,0:T(8,128)}, u32[]{:S(2)}) copy-start(f32[32,512]{1,0:T(8,128)} %mom_q.1) | copy-start | bytes 196612
  0.7 39.2 %copy-start.2 = (f32[512,32]{0,1:T(8,128)S(1)}, f32[512,32]{0,1:T(8,128)}, u32[]{:S(2)}) copy-start(f32[512,32]{0,1:T(8,128)} %param.23) | copy-start | bytes 196612
  0.7 39.2 %copy-start.3 = (f32[512,32]{0,1:T(8,128)S(1)}, f32[512,32]{0,1:T(8,128)}, u32[]{:S(2)}) copy-start(f32[512,32]{0,1:T(8,128)} %param.24) | copy-start | bytes 196612

commit v4 on v3

--- a/solution.py
+++ b/solution.py
@@ -217,9 +217,6 @@
     small_copies[0].wait()
     small_copies[1].wait()
     wo[...] = fold_gram(gio_v[...], fo_v[...]).T
-    small_copies[2].wait()
-    small_copies[3].wait()
-    wq[...] = fold_gram(giq_v[...], fq_v[...])
     for i in range(2):
         part = project_nn(mo[load_sum(i, mo), :], wo[...])
         for j in range(2):
@@ -230,6 +227,9 @@
     pl.semaphore_wait(barrier, n_others)
     a_send(0, 1, A_FAR)
 
+    small_copies[2].wait()
+    small_copies[3].wait()
+    wq[...] = fold_gram(giq_v[...], fq_v[...])
     for i in range(NY):
         part = project(mq[load_sum(2 + i, mq), :], wq[...])
         for c in range(NC):
@@ -280,16 +280,19 @@
 
     sum_z(0, 1, None)
 
+    sum_z(0, 0, None)
+
     wait_seven(gath, 0, 1, sem_gr)
     left = narrow(ga1.at[0])
     o_cols = mo.shape[1] // NA
-    for d in range(NA):
-        part = jnp.dot(left, mo[:, d * o_cols : (d + 1) * o_cols], preferred_element_type=f32).astype(bf16)
-        for t, tile in enumerate(wide_tiles(part)):
-            sa0[1, d, t] = tile
-    a_send(1, 0, A_FAR)
-
-    sum_z(0, 0, None)
+    for dy in Y_FAR:
+        d = ((y + dy) % NY) * NC
+        cols = pl.ds(pl.multiple_of(d * o_cols, NC * o_cols), NC * o_cols)
+        part = jnp.dot(left, mo[:, cols], preferred_element_type=f32).astype(bf16)
+        for c in range(NC):
+            for t, tile in enumerate(wide_tiles(part[:, c * o_cols : (c + 1) * o_cols])):
+                sa0[1, d + c, t] = tile
+        a_send(1, 0, [off for off in A_FAR if off[0] == dy])
 
     norm_wait(nz, NZ - 1, nsem_r.at[1])
     ntotal = nz[0]
@@ -297,8 +300,6 @@
         ntotal = ntotal + nz[k]
     nx[ten] = ntotal
     norm_send(nx.at[ten], nx.at[ten], 2, x_devices)
-
-    sum_a(1, 0)
 
     chunk = mq.shape[0] // NA
     wait_seven(gath, 0, 0, sem_gr)
@@ -308,6 +309,8 @@
         h, j = d // 4, d % 4
         sa1[1, d] = acc[h * 16 : h * 16 + 16, j * 128 : j * 128 + 128]
     a_send(1, 1, A_FAR)
+
+    sum_a(1, 0)
 
     gp_out[:, 0:4] = ga0[0]
     gp_out[:, 4] = ga1[0]

time: 42.6 us -> 40 us (0.939)
  Pallas kernels: 41.8 us -> 39.2 us
    pallas_call x1, Pallas kernels: 39.2 us -> 36.6 us  [on_device(): pl.pallas_call(functools.partial(reduce_kernel, replicas, replicas * tens...]
where the time goes in v4:
time: 40 us; the launch traced here: 39.9 us
  Pallas kernels  39.2 us (98%)
  between operations  0.72 us (2%)
    pallas_call x1, Pallas kernels, on_device(): pl.pallas_call(functools.partial(reduce_kernel, replicas, replicas * tens...  36.6 us
    pallas_call x1, Pallas kernels, on_device(): pl.pallas_call(update_kernel, out_shape=(jax.ShapeDtypeStruct(shape_q, bf...  2.56 us

profile of v4, /device:TPU:1, one launch (start us, length us, event | category | flops | bytes accessed | tf_op | source)
XLA Modules:
  0.0 39.9 jit_solution(15296905799421431685)
XLA Ops:
  0.6 0.0 copy-start
  0.7 0.0 copy-start.1
  0.7 0.0 copy-start.2
  0.7 0.0 copy-start.3
  0.7 36.6 %reduce_factors.1 = (bf16[2048,512]{1,0:T(8,128)(2,1)S(1)}, bf16[512,2048]{1,0:T(8,128)(2,1)S(1)}, bf16[8,5,16,128]{3,2,1,0:T(8,128)(2,1)S(1)}, bf16[8,5,16,128]{3,2,1,0:T(8,128)(2,1)S(1)}, f32[1,4096]{1,0:T(1,128)S(1)}) custom-call(bf16[2048,512]{1,0:T(8,128)(2,1)} %gq.1, bf16[2048,512]{1,0:T(8,128)(2,1)} %eq.1, bf16[512,2048]{1,0:T(8,128)(2,1)} %go.1, ...), custom_call_target="tpu_custom_call" | custom-call | tf_op jit(solution)/shard_map/reduce_factors/pallas_call | solution.py:425
  37.3 0.0 copy-done
  37.3 0.0 copy-done.1
  37.3 0.0 copy-done.2
  37.3 0.0 copy-done.3
  37.3 2.6 %apply_update.1 = (bf16[2048,512]{1,0:T(8,128)(2,1)}, bf16[512,2048]{1,0:T(8,128)(2,1)}, bf16[32,512]{1,0:T(8,128)(2,1)}, bf16[32,2048]{1,0:T(8,128)(2,1)}, f32[...) custom-call(bf16[8,5,16,128]{3,2,1,0:T(8,128)(2,1)S(1)} %get-tuple-element., ...), custom_call_target="tpu_custom_call" | custom-call | tf_op jit(solution)/shard_map/apply_update/pallas_call | solution.py:470
Async XLA Ops:
  0.6 36.6 %copy-start = (f32[32,512]{1,0:T(8,128)S(1)}, f32[32,512]{1,0:T(8,128)}, u32[]{:S(2)}) copy-start(f32[32,512]{1,0:T(8,128)} %wq.1) | copy-start | bytes 196612
  0.7 36.6 %copy-start.1 = (f32[32,512]{1,0:T(8,128)S(1)}, f32[32,512]{1,0:T(8,128)}, u32[]{:S(2)}) copy-start(f32[32,512]{1,0:T(8,128)} %mom_q.1) | copy-start | bytes 196612
  0.7 36.6 %copy-start.2 = (f32[512,32]{0,1:T(8,128)S(1)}, f32[512,32]{0,1:T(8,128)}, u32[]{:S(2)}) copy-start(f32[512,32]{0,1:T(8,128)} %param.23) | copy-start | bytes 196612
  0.7 36.6 %copy-start.3 = (f32[512,32]{0,1:T(8,128)S(1)}, f32[512,32]{0,1:T(8,128)}, u32[]{:S(2)}) copy-start(f32[512,32]{0,1:T(8,128)} %param.24) | copy-start | bytes 196612
